TPU v7x, 32 devices: a whole 2x2x4 slice. The times are simulated.
32 devices in a mesh: gx: 4 (over y, core), gy: 2 (over x), ch: 4 (over z).
Axes of the slice: x: 2, y: 2, z: 4, core: 2. Of those that a mesh axis runs over, the one named last changes fastest.
Arguments:
- density: bfloat16 [4, 32, 128, 128], P('gx', 'gy', 'ch'), may hold values from -6 to 6
- first_kernel: bfloat16 [3, 3, 3, 128, 128], P(None, None, None, 'ch'), may hold values from -0.109375 to 0.109375
- first_bias: float32 [128], P('ch'), may hold values from -3 to 3
- second_kernel: bfloat16 [3, 3, 3, 128, 128], P(None, None, None, 'ch'), may hold values from -0.109375 to 0.109375
- second_bias: float32 [128], P('ch'), may hold values from -3 to 3
Outputs:
- features: bfloat16 [4, 32, 128, 128], P('gx', 'gy', 'ch')
All inputs are finite; a program needn't handle non-finite values.
Results may differ from a plain program's by a relative error of at most 0.0045.
Values may be sent and summed in bfloat16 or wider, within the bound.
No kernel may reach another device: no remote copies, remote signals or barrier semaphores. Data moves between devices by JAX's collectives and lax.ppermute only.
A program may use at most 64 MiB of HBM per device.

v0:
```python
import jax
import jax.numpy as jnp
from jax import lax
from jax.sharding import PartitionSpec as P


def with_halo(block, sides, width):
    for axis, dim in sides:
        count = lax.axis_size(axis)
        forward = [(i, i + 1) for i in range(count - 1)]
        backward = [(target, source) for source, target in forward]
        low = lax.ppermute(
            lax.slice_in_dim(block, block.shape[dim] - width, None, axis=dim), axis, forward
        )
        high = lax.ppermute(lax.slice_in_dim(block, 0, width, axis=dim), axis, backward)
        block = jnp.concatenate([low, block, high], axis=dim)
    return block


def conv_taps(padded, kernel):
    result = lax.conv_general_dilated(
        padded[None],
        kernel,
        (1, 1, 1),
        "VALID",
        dimension_numbers=("NHWCD", "HWDOI", "NHWCD"),
        preferred_element_type=jnp.float32,
    )
    return result[0]


def finish(total, bias):
    return jnp.maximum(total + bias.reshape(1, 1, -1, 1), 0.0).astype(jnp.bfloat16)


def pad_depth(field):
    return jnp.pad(field, ((0, 0), (0, 0), (0, 0), (1, 1)))


def layer_channels(field, kernel, bias):
    whole = lax.all_gather(field, "ch", axis=2, tiled=True)
    padded = with_halo(pad_depth(whole), (("gx", 0), ("gy", 1)), 1)
    total = conv_taps(padded, kernel)
    return finish(total, bias)


def per_device(density, first_kernel, first_bias, second_kernel, second_bias):
    hidden = layer_channels(density, first_kernel, first_bias)
    return layer_channels(hidden, second_kernel, second_bias)


def solution(mesh):
    placed = (
        P("gx", "gy", "ch", None),
        P(None, None, None, "ch", None),
        P("ch"),
        P(None, None, None, "ch", None),
        P("ch"),
    )
    return jax.shard_map(
        per_device, mesh=mesh, in_specs=placed, out_specs=P("gx", "gy", "ch", None), check_vma=False
    )
```

profile of v0, /device:TPU:12, one launch (start us, length us, event | category | flops | bytes accessed | tf_op | source)
XLA Modules:
  0.0 126.0 jit_solution(12742077173878891672)
XLA Ops:
  1.0 16.5 %all_gather.6 = bf16[1,16,128,128]{3,1,0,2:T(8,128)(2,1)S(1)} all-gather(bf16[1,16,32,128]{3,1,0,2:T(8,128)(2,1)S(1)} %copy.78), channel_id=1, replica_groups=mesh['gx'=4,'gy'=2,'ch'=4] {'ch'}, dimensions={2}, use_global_device_ids=true | all-gather | bytes 655360 | tf_op jit(solution)/shard_map/all_gather | solution.py:41
  19.1 1.9 %collective-permute-start.1 = (bf16[1,16,128,130]{2,1,3,0:T(8,128)(2,1)S(1)}, bf16[1,16,128,130]{2,1,3,0:T(8,128)(2,1)S(1)}, u32[]{:S(2)}, u32[]{:S(2)}) collective-permute-start(bf16[1,16,128,130]{2,1,3,0:T(8,128)(2,1)S(1)} %copy.79), channel_id=1, source_target_pairs={{8,0},{16,8},{24,16},{9,1},{17,9},{25,17},{10,2},{18,10},{26,18},{... | collective-permute-start | bytes 1597448 | tf_op jit(solution)/shard_map/ppermute | solution.py:15
  21.0 2.4 %collective-permute-start = (bf16[1,16,128,130]{2,1,3,0:T(8,128)(2,1)S(1)}, bf16[1,16,128,130]{2,1,3,0:T(8,128)(2,1)S(1)}, u32[]{:S(2)}, u32[]{:S(2)}) collective-permute-start(bf16[1,16,128,130]{2,1,3,0:T(8,128)(2,1)S(1)} %copy.79), channel_id=1, source_target_pairs={{0,8},{8,16},{16,24},{1,9},{9,17},{17,25},{2,10},{10,18},{18,26},{... | collective-permute-start | bytes 1597448 | tf_op jit(solution)/shard_map/ppermute | solution.py:12
  23.4 4.3 %collective-permute-done.1 = bf16[1,16,128,130]{2,1,3,0:T(8,128)(2,1)S(1)} collective-permute-done((bf16[1,16,128,130]{2,1,3,0:T(8,128)(2,1)S(1)}, bf16[1,16,128,130]{2,1,3,0:T(8,128)(2,1)S(1)}, u32[]{:S(2)}, u32[]{:S(2)}) %collective-permute-start.1) | collective-permute-done | bytes 532512 | tf_op jit(solution)/shard_map/ppermute | solution.py:15
  27.8 1.8 %copy.82 = bf16[1,16,128,130]{3,1,0,2:T(8,128)(2,1)} copy(bf16[1,16,128,130]{2,1,3,0:T(8,128)(2,1)S(1)} %collective-permute-done.1) | data formatting | bytes 1064960 | tf_op jit(solution)/shard_map/ppermute | solution.py:15
  29.6 2.0 %collective-permute-done = bf16[1,16,128,130]{2,1,3,0:T(8,128)(2,1)S(1)} collective-permute-done((bf16[1,16,128,130]{2,1,3,0:T(8,128)(2,1)S(1)}, bf16[1,16,128,130]{2,1,3,0:T(8,128)(2,1)S(1)}, u32[]{:S(2)}, u32[]{:S(2)}) %collective-permute-start) | collective-permute-done | bytes 532512 | tf_op jit(solution)/shard_map/ppermute | solution.py:12
  31.6 1.8 %copy.81 = bf16[1,16,128,130]{3,1,0,2:T(8,128)(2,1)} copy(bf16[1,16,128,130]{2,1,3,0:T(8,128)(2,1)S(1)} %collective-permute-done) | data formatting | bytes 1064960 | tf_op jit(solution)/shard_map/ppermute | solution.py:12
  33.4 2.4 %pad_maximum_fusion = bf16[3,16,128,130]{3,1,0,2:T(8,128)(2,1)S(1)} fusion(bf16[1,16,128,130]{3,1,0,2:T(8,128)(2,1)} %copy.82, bf16[1,16,128,130]{3,1,0,2:T(8,128)(2,1)} %copy-done.1, bf16[1,16,128,130]{3,1,0,2:T(8,128)(2,1)} %copy.81), kind=kLoop, calls=%fused_computation.3 | loop fusion | flops 1597440 | bytes 3194880 | tf_op jit(solution)/shard_map/concatenate | solution.py:16
  41.6 5.8 %collective-permute-start.2 = (bf16[3,1,128,130]{2,3,1,0:T(8,128)(2,1)S(1)}, bf16[3,1,128,130]{2,3,1,0:T(8,128)(2,1)}, u32[]{:S(2)}, u32[]{:S(2)}) collective-permute-start(bf16[3,1,128,130]{2,3,1,0:T(8,128)(2,1)S(1)} %copy.83), channel_id=1, source_target_pairs={{0,4},{1,5},{2,6},{3,7},{8,12},{9,13},{10,14},{11,15},{16,20},{17,... | collective-permute-start | bytes 299528 | tf_op jit(solution)/shard_map/ppermute | solution.py:12
  47.5 3.2 %copy.85 = bf16[3,16,128,130]{2,3,1,0:T(8,128)(2,1)} copy(bf16[3,16,128,130]{3,1,0,2:T(8,128)(2,1)S(1)} %pad_maximum_fusion) | data formatting | bytes 3194880 | tf_op jit(solution)/shard_map/concatenate | solution.py:16
  53.8 3.3 %reshape.50 = bf16[3,18,128,1,8,17]{2,5,4,1,0,3:T(8,128)(2,1)S(1)} reshape(bf16[3,18,128,1,136]{2,4,1,0,3:T(8,128)(2,1)} %pad.9) | data formatting | bytes 3760128 | tf_op jit(solution)/shard_map/conv_general_dilated | solution.py:21
  57.8 4.2 %fusion.19 = f32[1,16,8,17,32]{4,2,3,1,0:T(8,128)S(1)} fusion(bf16[3,3,3,32,128]{4,3,2,1,0:T(8,128)(2,1)S(1)} %copy-done, bf16[3,18,128,1,7,2]{2,4,5,1,0,3:T(8,128)(2,1)S(1)} %slice.22, bf16[3,18,128,1,8,17]{2,4,5,1,0,3:T(8,128)(2,1)S(1)} %copy.87, pred[8,17]{0,1:T(8,128)(4,1)S(1)} %copy-done.6), kind=kOutput, calls=%fused_computation.20 | convolution fusion | flops 487669760 | bytes 2573448 | tf_op jit(solution)/shard_map/conv_general_dilated | solution.py:21
  63.1 15.0 %all_gather.7 = bf16[1,16,128,128]{3,1,0,2:T(8,128)(2,1)S(1)} all-gather(bf16[1,16,32,128]{3,1,0,2:T(8,128)(2,1)S(1)} %copy.90), channel_id=1, replica_groups=mesh['gx'=4,'gy'=2,'ch'=4] {'ch'}, dimensions={2}, use_global_device_ids=true | all-gather | bytes 655360 | tf_op jit(solution)/shard_map/all_gather | solution.py:41
  79.7 1.9 %collective-permute-start.5 = (bf16[1,16,128,130]{2,1,3,0:T(8,128)(2,1)S(1)}, bf16[1,16,128,130]{2,1,3,0:T(8,128)(2,1)S(1)}, u32[]{:S(2)}, u32[]{:S(2)}) collective-permute-start(bf16[1,16,128,130]{2,1,3,0:T(8,128)(2,1)S(1)} %copy.91), channel_id=1, source_target_pairs={{8,0},{16,8},{24,16},{9,1},{17,9},{25,17},{10,2},{18,10},{26,18},{... | collective-permute-start | bytes 1597448 | tf_op jit(solution)/shard_map/ppermute | solution.py:15
  81.6 2.6 %collective-permute-start.4 = (bf16[1,16,128,130]{2,1,3,0:T(8,128)(2,1)S(1)}, bf16[1,16,128,130]{2,1,3,0:T(8,128)(2,1)S(1)}, u32[]{:S(2)}, u32[]{:S(2)}) collective-permute-start(bf16[1,16,128,130]{2,1,3,0:T(8,128)(2,1)S(1)} %copy.91), channel_id=1, source_target_pairs={{0,8},{8,16},{16,24},{1,9},{9,17},{17,25},{2,10},{10,18},{18,26},{... | collective-permute-start | bytes 1597448 | tf_op jit(solution)/shard_map/ppermute | solution.py:12
  84.2 4.1 %collective-permute-done.5 = bf16[1,16,128,130]{2,1,3,0:T(8,128)(2,1)S(1)} collective-permute-done((bf16[1,16,128,130]{2,1,3,0:T(8,128)(2,1)S(1)}, bf16[1,16,128,130]{2,1,3,0:T(8,128)(2,1)S(1)}, u32[]{:S(2)}, u32[]{:S(2)}) %collective-permute-start.5) | collective-permute-done | bytes 532512 | tf_op jit(solution)/shard_map/ppermute | solution.py:15
  90.2 2.0 %collective-permute-done.4 = bf16[1,16,128,130]{2,1,3,0:T(8,128)(2,1)S(1)} collective-permute-done((bf16[1,16,128,130]{2,1,3,0:T(8,128)(2,1)S(1)}, bf16[1,16,128,130]{2,1,3,0:T(8,128)(2,1)S(1)}, u32[]{:S(2)}, u32[]{:S(2)}) %collective-permute-start.4) | collective-permute-done | bytes 532512 | tf_op jit(solution)/shard_map/ppermute | solution.py:12
  92.2 1.8 %copy.93 = bf16[1,16,128,130]{3,1,0,2:T(8,128)(2,1)} copy(bf16[1,16,128,130]{2,1,3,0:T(8,128)(2,1)S(1)} %collective-permute-done.4) | data formatting | bytes 1064960 | tf_op jit(solution)/shard_map/ppermute | solution.py:12
  94.0 2.4 %pad_maximum_fusion.1 = bf16[3,16,128,130]{3,1,0,2:T(8,128)(2,1)S(1)} fusion(bf16[1,16,128,130]{3,1,0,2:T(8,128)(2,1)} %copy.94, bf16[1,16,128,130]{3,1,0,2:T(8,128)(2,1)} %copy-done.2, bf16[1,16,128,130]{3,1,0,2:T(8,128)(2,1)} %copy.93), kind=kLoop, calls=%fused_computation.4 | loop fusion | flops 1597440 | bytes 3194880 | tf_op jit(solution)/shard_map/concatenate | solution.py:16
  98.0 3.6 %collective-permute-start.6 = (bf16[3,1,128,130]{3,1,0,2:T(2,128)(2,1)}, bf16[3,1,128,130]{3,1,0,2:T(2,128)(2,1)}, u32[]{:S(2)}, u32[]{:S(2)}) collective-permute-start(bf16[3,1,128,130]{3,1,0,2:T(2,128)(2,1)} %get-tuple-element.5), channel_id=1, source_target_pairs={{0,4},{1,5},{2,6},{3,7},{8,12},{9,13},{10,14},{11,15},{16,20},{17,... | collective-permute-start | bytes 299528 | tf_op jit(solution)/shard_map/ppermute | solution.py:12
  102.9 3.2 %copy.96 = bf16[3,16,128,130]{2,3,1,0:T(8,128)(2,1)} copy(bf16[3,16,128,130]{3,1,0,2:T(8,128)(2,1)S(1)} %pad_maximum_fusion.1) | data formatting | bytes 3194880 | tf_op jit(solution)/shard_map/concatenate | solution.py:16
  107.7 3.9 %collective-permute-done.7 = bf16[3,1,128,130]{3,1,0,2:T(2,128)(2,1)} collective-permute-done((bf16[3,1,128,130]{3,1,0,2:T(2,128)(2,1)}, bf16[3,1,128,130]{3,1,0,2:T(2,128)(2,1)}, u32[]{:S(2)}, u32[]{:S(2)}) %collective-permute-start.7) | collective-permute-done | bytes 99872 | tf_op jit(solution)/shard_map/ppermute | solution.py:15
  115.9 3.3 %reshape.57 = bf16[3,18,128,1,8,17]{2,5,4,1,0,3:T(8,128)(2,1)S(1)} reshape(bf16[3,18,128,1,136]{2,4,1,0,3:T(8,128)(2,1)} %pad.11) | data formatting | bytes 3760128 | tf_op jit(solution)/shard_map/conv_general_dilated | solution.py:21
  120.2 4.2 %fusion.16 = f32[1,16,8,17,32]{4,2,3,1,0:T(8,128)S(1)} fusion(bf16[3,3,3,32,128]{4,3,2,1,0:T(8,128)(2,1)S(1)} %copy-done.5, bf16[3,18,128,1,7,2]{2,4,5,1,0,3:T(8,128)(2,1)S(1)} %slice.26, bf16[3,18,128,1,8,17]{2,4,5,1,0,3:T(8,128)(2,1)S(1)} %copy.99, pred[8,17]{0,1:T(8,128)(4,1)S(1)} %copy-done.6), kind=kOutput, calls=%fused_computation.19 | convolution fusion | flops 487669760 | bytes 2573448 | tf_op jit(solution)/shard_map/conv_general_dilated | solution.py:21
  (48 shorter events, 27.8 us)
Async XLA Ops:
  0.0 57.5 %copy-start = (bf16[3,3,3,32,128]{4,3,2,1,0:T(8,128)(2,1)S(1)}, bf16[3,3,3,32,128]{4,3,2,1,0:T(8,128)(2,1)}, u32[]{:S(2)}) copy-start(bf16[3,3,3,32,128]{4,3,2,1,0:T(8,128)(2,1)} %param.6) | copy-start | bytes 663556
  17.9 13.7 %copy-start.1 = (bf16[1,16,128,130]{3,1,0,2:T(8,128)(2,1)}, bf16[1,16,128,130]{3,1,0,2:T(8,128)(2,1)S(1)}, u32[]{:S(2)}) copy-start(bf16[1,16,128,130]{3,1,0,2:T(8,128)(2,1)S(1)} %pad.7) | copy-start | bytes 1597444
  19.1 8.7 %collective-permute-start.1 = (bf16[1,16,128,130]{2,1,3,0:T(8,128)(2,1)S(1)}, bf16[1,16,128,130]{2,1,3,0:T(8,128)(2,1)S(1)}, u32[]{:S(2)}, u32[]{:S(2)}) collective-permute-start(bf16[1,16,128,130]{2,1,3,0:T(8,128)(2,1)S(1)} %copy.79), channel_id=1, source_target_pairs={{8,0},{16,8},{24,16},{9,1},{17,9},{25,17},{10,2},{18,10},{26,18},{... | collective-permute-start | bytes 1597448 | tf_op jit(solution)/shard_map/ppermute | solution.py:15
  21.0 10.6 %collective-permute-start = (bf16[1,16,128,130]{2,1,3,0:T(8,128)(2,1)S(1)}, bf16[1,16,128,130]{2,1,3,0:T(8,128)(2,1)S(1)}, u32[]{:S(2)}, u32[]{:S(2)}) collective-permute-start(bf16[1,16,128,130]{2,1,3,0:T(8,128)(2,1)S(1)} %copy.79), channel_id=1, source_target_pairs={{0,8},{8,16},{16,24},{1,9},{9,17},{17,25},{2,10},{10,18},{18,26},{... | collective-permute-start | bytes 1597448 | tf_op jit(solution)/shard_map/ppermute | solution.py:12
  40.4 10.3 %collective-permute-start.3 = (bf16[3,1,128,130]{2,3,1,0:T(8,128)(2,1)}, bf16[3,1,128,130]{2,3,1,0:T(8,128)(2,1)}, u32[]{:S(2)}, u32[]{:S(2)}) collective-permute-start(bf16[3,1,128,130]{2,3,1,0:T(8,128)(2,1)} %copy.84), channel_id=1, source_target_pairs={{4,0},{5,1},{6,2},{7,3},{12,8},{13,9},{14,10},{15,11},{20,16},{21,... | collective-permute-start | bytes 299528 | tf_op jit(solution)/shard_map/ppermute | solution.py:15
  41.6 9.0 %collective-permute-start.2 = (bf16[3,1,128,130]{2,3,1,0:T(8,128)(2,1)S(1)}, bf16[3,1,128,130]{2,3,1,0:T(8,128)(2,1)}, u32[]{:S(2)}, u32[]{:S(2)}) collective-permute-start(bf16[3,1,128,130]{2,3,1,0:T(8,128)(2,1)S(1)} %copy.83), channel_id=1, source_target_pairs={{0,4},{1,5},{2,6},{3,7},{8,12},{9,13},{10,14},{11,15},{16,20},{17,... | collective-permute-start | bytes 299528 | tf_op jit(solution)/shard_map/ppermute | solution.py:12
  57.1 0.7 copy-start.6
  62.3 0.7 copy-start.3
  78.5 13.7 %copy-start.2 = (bf16[1,16,128,130]{3,1,0,2:T(8,128)(2,1)}, bf16[1,16,128,130]{3,1,0,2:T(8,128)(2,1)S(1)}, u32[]{:S(2)}) copy-start(bf16[1,16,128,130]{3,1,0,2:T(8,128)(2,1)S(1)} %pad.8) | copy-start | bytes 1597444
  79.7 8.7 %collective-permute-start.5 = (bf16[1,16,128,130]{2,1,3,0:T(8,128)(2,1)S(1)}, bf16[1,16,128,130]{2,1,3,0:T(8,128)(2,1)S(1)}, u32[]{:S(2)}, u32[]{:S(2)}) collective-permute-start(bf16[1,16,128,130]{2,1,3,0:T(8,128)(2,1)S(1)} %copy.91), channel_id=1, source_target_pairs={{8,0},{16,8},{24,16},{9,1},{17,9},{25,17},{10,2},{18,10},{26,18},{... | collective-permute-start | bytes 1597448 | tf_op jit(solution)/shard_map/ppermute | solution.py:15
  81.6 10.6 %collective-permute-start.4 = (bf16[1,16,128,130]{2,1,3,0:T(8,128)(2,1)S(1)}, bf16[1,16,128,130]{2,1,3,0:T(8,128)(2,1)S(1)}, u32[]{:S(2)}, u32[]{:S(2)}) collective-permute-start(bf16[1,16,128,130]{2,1,3,0:T(8,128)(2,1)S(1)} %copy.91), channel_id=1, source_target_pairs={{0,8},{8,16},{16,24},{1,9},{9,17},{17,25},{2,10},{10,18},{18,26},{... | collective-permute-start | bytes 1597448 | tf_op jit(solution)/shard_map/ppermute | solution.py:12
  98.0 8.4 %collective-permute-start.6 = (bf16[3,1,128,130]{3,1,0,2:T(2,128)(2,1)}, bf16[3,1,128,130]{3,1,0,2:T(2,128)(2,1)}, u32[]{:S(2)}, u32[]{:S(2)}) collective-permute-start(bf16[3,1,128,130]{3,1,0,2:T(2,128)(2,1)} %get-tuple-element.5), channel_id=1, source_target_pairs={{0,4},{1,5},{2,6},{3,7},{8,12},{9,13},{10,14},{11,15},{16,20},{17,... | collective-permute-start | bytes 299528 | tf_op jit(solution)/shard_map/ppermute | solution.py:12
  101.6 10.0 %collective-permute-start.7 = (bf16[3,1,128,130]{3,1,0,2:T(2,128)(2,1)}, bf16[3,1,128,130]{3,1,0,2:T(2,128)(2,1)}, u32[]{:S(2)}, u32[]{:S(2)}) collective-permute-start(bf16[3,1,128,130]{3,1,0,2:T(2,128)(2,1)} %get-tuple-element.6), channel_id=1, source_target_pairs={{4,0},{5,1},{6,2},{7,3},{12,8},{13,9},{14,10},{15,11},{20,16},{21,... | collective-permute-start | bytes 299528 | tf_op jit(solution)/shard_map/ppermute | solution.py:15
  119.2 0.9 copy-start.5
  124.6 0.7 copy-start.4
where the time goes:
time: 127 us; the launch traced here: 126 us
  local copies, waits for them, and re-layouts  39.1 us (31%)
  blocking collectives  31.4 us (25%)
  starting transfers between devices  20.9 us (16%)
  waiting for transfers between devices  16.7 us (13%)
  other arithmetic  9.15 us (7%)
  matrix products  8.49 us (7%)
    all_gather x2, blocking collectives, layer_channels(): whole = lax.all_gather(field, 'ch', axis=2, tiled=True)  31.4 us
    ppermute x4, starting transfers between devices, with_halo(): lax.ppermute(lax.slice_in_dim(block, block.shape[dim] - width, None, axis...  14.5 us
    ppermute x4, waiting for transfers between devices, with_halo(): lax.ppermute(lax.slice_in_dim(block, 0, width, axis=dim), axis, backward)  12.4 us
    conv_general_dilated x2, matrix products, conv_taps(): lax.conv_general_dilated(padded[None], kernel, (1, 1, 1), 'VALID', dimens...  8.49 us
    conv_general_dilated x10, local copies, waits for them, and re-layouts, conv_taps(): lax.conv_general_dilated(padded[None], kernel, (1, 1, 1), 'VALID', dimens...  7.88 us
    ppermute x4, starting transfers between devices, with_halo(): lax.ppermute(lax.slice_in_dim(block, 0, width, axis=dim), axis, backward)  6.4 us
    concatenate x2, local copies, waits for them, and re-layouts, with_halo(): block = jnp.concatenate([low, block, high], axis=dim)  6.33 us
    ppermute x3, local copies, waits for them, and re-layouts, with_halo(): lax.ppermute(lax.slice_in_dim(block, block.shape[dim] - width, None, axis...  4.91 us
  transfers between devices with their start and end apart: 8, of which 6 were waited for; matrix products, arithmetic and copies ran while one was open for 9% of the time, Pallas kernels for 0%

commit v1 on v0

--- a/solution.py
+++ b/solution.py
@@ -2,6 +2,28 @@
 import jax.numpy as jnp
 from jax import lax
 from jax.sharding import PartitionSpec as P
+
+
+def joined_along(blocks, dim):
+    blocks = jnp.moveaxis(blocks, 0, dim)
+    shape = blocks.shape
+    return blocks.reshape(*shape[:dim], shape[dim] * shape[dim + 1], *shape[dim + 2 :])
+
+
+def ring_gather(x, axis, dim):
+    peers = lax.axis_size(axis)
+    pairs = [(i, (i + 1) % peers) for i in range(peers)]
+    back = [(b, a) for a, b in pairs]
+    lower, upper = ([], [])
+    for hop in range(peers - 1):
+        if hop % 2 == 0:
+            lower.append(lax.ppermute(lower[-1] if lower else x, axis, pairs))
+        else:
+            upper.append(lax.ppermute(upper[-1] if upper else x, axis, back))
+    pieces = jnp.stack([*lower[::-1], x, *upper])
+    shift = lax.axis_index(axis) - len(lower)
+    pieces = pieces[(jnp.arange(peers) - shift) % peers]
+    return joined_along(pieces, dim)
 
 
 def with_halo(block, sides, width):
@@ -38,7 +60,7 @@
 
 
 def layer_channels(field, kernel, bias):
-    whole = lax.all_gather(field, "ch", axis=2, tiled=True)
+    whole = ring_gather(field, "ch", 2)
     padded = with_halo(pad_depth(whole), (("gx", 0), ("gy", 1)), 1)
     total = conv_taps(padded, kernel)
     return finish(total, bias)

time: 127 us -> 117 us (0.921)
  the two profiles are of different devices: /device:TPU:12 before, /device:TPU:4 now
where the time goes in v1:
time: 117 us
  waiting for transfers between devices  48 us (41%)
  local copies, waits for them, and re-layouts  28.7 us (25%)
  starting transfers between devices  24.1 us (21%)
  matrix products  8.49 us (7%)
  other arithmetic  6.7 us (6%)
    ppermute x4, waiting for transfers between devices, ring_gather(): lower.append(lax.ppermute(lower[-1] if lower else x, axis, pairs))  19.3 us
    ppermute x4, waiting for transfers between devices, with_halo(): lax.ppermute(lax.slice_in_dim(block, 0, width, axis=dim), axis, backward)  17.5 us
    ppermute x4, waiting for transfers between devices, with_halo(): lax.ppermute(lax.slice_in_dim(block, block.shape[dim] - width, None, axis...  10.2 us
    unnamed x14, local copies, waits for them, and re-layouts  9.85 us
    ppermute x4, starting transfers between devices, with_halo(): lax.ppermute(lax.slice_in_dim(block, block.shape[dim] - width, None, axis...  9.85 us
    conv_general_dilated x2, matrix products, conv_taps(): lax.conv_general_dilated(padded[None], kernel, (1, 1, 1), 'VALID', dimens...  8.49 us
    conv_general_dilated x10, local copies, waits for them, and re-layouts, conv_taps(): lax.conv_general_dilated(padded[None], kernel, (1, 1, 1), 'VALID', dimens...  7.88 us
    ppermute x4, starting transfers between devices, with_halo(): lax.ppermute(lax.slice_in_dim(block, 0, width, axis=dim), axis, backward)  6.61 us
  transfers between devices with their start and end apart: 14, of which 13 were waited for; matrix products, arithmetic and copies ran while one was open for 2% of the time, Pallas kernels for 0%

profile of v1, /device:TPU:4, one launch (start us, length us, event | category | flops | bytes accessed | tf_op | source)
XLA Modules:
  0.0 116.5 jit_solution(18308567674322929433)
XLA Ops:
  1.6 2.2 %collective-permute-start.2 = (bf16[1,16,32,128]{3,2,1,0:T(8,128)(2,1)}, bf16[1,16,32,128]{3,2,1,0:T(8,128)(2,1)S(1)}, u32[]{:S(2)}, u32[]{:S(2)}) collective-permute-start(bf16[1,16,32,128]{3,2,1,0:T(8,128)(2,1)} %param.5), channel_id=1, source_target_pairs={{1,0},{2,1},{3,2},{0,3},{5,4},{6,5},{7,6},{4,7},{9,8},{10,9},{11,1... | collective-permute-start | bytes 393224 | tf_op jit(solution)/shard_map/ppermute | solution.py:22
  3.8 4.6 %collective-permute-done = bf16[1,16,32,128]{3,2,1,0:T(8,128)(2,1)S(1)} collective-permute-done((bf16[1,16,32,128]{3,2,1,0:T(8,128)(2,1)}, bf16[1,16,32,128]{3,2,1,0:T(8,128)(2,1)S(1)}, u32[]{:S(2)}, u32[]{:S(2)}) %collective-permute-start) | collective-permute-done | bytes 131104 | tf_op jit(solution)/shard_map/ppermute | solution.py:20
  9.6 5.6 %collective-permute-done.1 = bf16[1,16,32,128]{3,2,1,0:T(8,128)(2,1)S(1)} collective-permute-done((bf16[1,16,32,128]{3,2,1,0:T(8,128)(2,1)S(1)}, bf16[1,16,32,128]{3,2,1,0:T(8,128)(2,1)S(1)}, u32[]{:S(2)}, u32[]{:S(2)}) %collective-permute-start.1) | collective-permute-done | bytes 131104 | tf_op jit(solution)/shard_map/ppermute | solution.py:20
  19.8 2.4 %collective-permute-start.3 = (bf16[1,16,128,130]{2,1,3,0:T(8,128)(2,1)S(1)}, bf16[1,16,128,130]{2,1,3,0:T(8,128)(2,1)}, u32[]{:S(2)}, u32[]{:S(2)}) collective-permute-start(bf16[1,16,128,130]{2,1,3,0:T(8,128)(2,1)S(1)} %copy.87), channel_id=1, source_target_pairs={{0,8},{8,16},{16,24},{1,9},{9,17},{17,25},{2,10},{10,18},{18,26},{... | collective-permute-start | bytes 1597448 | tf_op jit(solution)/shard_map/ppermute | solution.py:34
  22.3 4.3 %collective-permute-done.4 = bf16[1,16,128,130]{2,1,3,0:T(8,128)(2,1)S(1)} collective-permute-done((bf16[1,16,128,130]{2,1,3,0:T(8,128)(2,1)S(1)}, bf16[1,16,128,130]{2,1,3,0:T(8,128)(2,1)S(1)}, u32[]{:S(2)}, u32[]{:S(2)}) %collective-permute-start.4) | collective-permute-done | bytes 532512 | tf_op jit(solution)/shard_map/ppermute | solution.py:37
  27.2 3.3 %collective-permute-done.3 = bf16[1,16,128,130]{2,1,3,0:T(8,128)(2,1)} collective-permute-done((bf16[1,16,128,130]{2,1,3,0:T(8,128)(2,1)S(1)}, bf16[1,16,128,130]{2,1,3,0:T(8,128)(2,1)}, u32[]{:S(2)}, u32[]{:S(2)}) %collective-permute-start.3) | collective-permute-done | bytes 532512 | tf_op jit(solution)/shard_map/ppermute | solution.py:34
  32.1 3.4 %collective-permute-start.5 = (bf16[3,1,128,130]{3,2,1,0:T(8,128)(2,1)S(1)}, bf16[3,1,128,130]{3,2,1,0:T(8,128)(2,1)S(1)}, u32[]{:S(2)}, u32[]{:S(2)}) collective-permute-start(bf16[3,1,128,130]{3,2,1,0:T(8,128)(2,1)S(1)} %get-tuple-element.7), channel_id=1, source_target_pairs={{0,4},{1,5},{2,6},{3,7},{8,12},{9,13},{10,14},{11,15},{16,20},{17,... | collective-permute-start | bytes 299528 | tf_op jit(solution)/shard_map/ppermute | solution.py:34
  38.7 4.4 %collective-permute-done.6 = bf16[3,1,128,130]{3,2,1,0:T(8,128)(2,1)S(1)} collective-permute-done((bf16[3,1,128,130]{3,2,1,0:T(8,128)(2,1)S(1)}, bf16[3,1,128,130]{3,2,1,0:T(8,128)(2,1)S(1)}, u32[]{:S(2)}, u32[]{:S(2)}) %collective-permute-start.6) | collective-permute-done | bytes 99872 | tf_op jit(solution)/shard_map/ppermute | solution.py:37
  43.1 2.3 %maximum_bitcast_fusion = bf16[3,18,128,1,130]{4,2,1,0,3:T(8,128)(2,1)} fusion(bf16[3,1,128,130]{3,2,1,0:T(8,128)(2,1)S(1)} %collective-permute-done.6, bf16[1,16,128,130]{3,2,1,0:T(8,128)(2,1)S(1)} %copy.90, bf16[1,16,128,130]{3,2,1,0:T(8,128)(2,1)S(1)} %pad.7, bf16[1,16,128,130]{3,2,1,0:T(8,128)(2,1)S(1)} %copy.89, ...), kind=kLoop, calls=%fused_computation.5 | loop fusion | flops 3594240 | bytes 3594240 | tf_op jit(solution)/shard_map/broadcast_in_dim | solution.py:44
  45.4 4.0 %copy.110 = bf16[3,18,128,1,130]{2,4,1,0,3:T(8,128)(2,1)S(1)} copy(bf16[3,18,128,1,130]{4,2,1,0,3:T(8,128)(2,1)} %maximum_bitcast_fusion) | data formatting | bytes 3594240
  50.8 3.3 %reshape.107 = bf16[3,18,128,1,8,17]{2,5,4,1,0,3:T(8,128)(2,1)S(1)} reshape(bf16[3,18,128,1,136]{2,4,1,0,3:T(8,128)(2,1)} %pad.9.clone) | data formatting | bytes 3760128 | tf_op jit(solution)/shard_map/conv_general_dilated | solution.py:43
  54.8 4.2 %maximum_convert_fusion = (bf16[1,16,8,17,32]{4,2,3,1,0:T(8,128)(2,1)S(1)}, f32[1,16,8,17,32]{4,2,3,1,0:T(8,128)S(1)}) fusion(f32[32]{0:T(128)S(1)} %copy-done.1, bf16[3,3,3,32,128]{4,3,2,1,0:T(8,128)(2,1)S(1)} %copy-done, bf16[3,18,128,1,7,2]{2,4,5,1,0,3:T(8,128)(2,1)S(1)} %slice.25, bf16[3,18,128,1,8,17]{2,4,5,1,0,3:T(8,128)(2,1)S(1)} %copy.93, ...), kind=kOutput, calls=%fused_computation.21 | convolution fusion | flops 487878656 | bytes 2712840 | tf_op jit(solution)/shard_map/conv_general_dilated | solution.py:43
  59.9 3.8 %collective-permute-start.9 = (bf16[1,16,32,128]{3,2,1,0:T(8,128)(2,1)S(1)}, bf16[1,16,32,128]{3,2,1,0:T(8,128)(2,1)S(1)}, u32[]{:S(2)}, u32[]{:S(2)}) collective-permute-start(bf16[1,16,32,128]{3,2,1,0:T(8,128)(2,1)S(1)} %fusion.27), channel_id=1, source_target_pairs={{1,0},{2,1},{3,2},{0,3},{5,4},{6,5},{7,6},{4,7},{9,8},{10,9},{11,1... | collective-permute-start | bytes 393224 | tf_op jit(solution)/shard_map/ppermute | solution.py:22
  63.8 2.9 %collective-permute-done.7 = bf16[1,16,32,128]{3,2,1,0:T(8,128)(2,1)S(1)} collective-permute-done((bf16[1,16,32,128]{3,2,1,0:T(8,128)(2,1)S(1)}, bf16[1,16,32,128]{3,2,1,0:T(8,128)(2,1)S(1)}, u32[]{:S(2)}, u32[]{:S(2)}) %collective-permute-start.7) | collective-permute-done | bytes 131104 | tf_op jit(solution)/shard_map/ppermute | solution.py:20
  67.2 6.3 %collective-permute-done.8 = bf16[1,16,32,128]{3,2,1,0:T(8,128)(2,1)S(1)} collective-permute-done((bf16[1,16,32,128]{3,2,1,0:T(8,128)(2,1)S(1)}, bf16[1,16,32,128]{3,2,1,0:T(8,128)(2,1)S(1)}, u32[]{:S(2)}, u32[]{:S(2)}) %collective-permute-start.8) | collective-permute-done | bytes 131104 | tf_op jit(solution)/shard_map/ppermute | solution.py:20
  75.3 1.9 %collective-permute-start.11 = (bf16[1,16,128,130]{2,1,3,0:T(8,128)(2,1)S(1)}, bf16[1,16,128,130]{2,1,3,0:T(8,128)(2,1)S(1)}, u32[]{:S(2)}, u32[]{:S(2)}) collective-permute-start(bf16[1,16,128,130]{2,1,3,0:T(8,128)(2,1)S(1)} %copy.99), channel_id=1, source_target_pairs={{8,0},{16,8},{24,16},{9,1},{17,9},{25,17},{10,2},{18,10},{26,18},{... | collective-permute-start | bytes 1597448 | tf_op jit(solution)/shard_map/ppermute | solution.py:37
  77.2 2.4 %collective-permute-start.10 = (bf16[1,16,128,130]{2,1,3,0:T(8,128)(2,1)S(1)}, bf16[1,16,128,130]{2,1,3,0:T(8,128)(2,1)}, u32[]{:S(2)}, u32[]{:S(2)}) collective-permute-start(bf16[1,16,128,130]{2,1,3,0:T(8,128)(2,1)S(1)} %copy.99), channel_id=1, source_target_pairs={{0,8},{8,16},{16,24},{1,9},{9,17},{17,25},{2,10},{10,18},{18,26},{... | collective-permute-start | bytes 1597448 | tf_op jit(solution)/shard_map/ppermute | solution.py:34
  79.7 4.3 %collective-permute-done.11 = bf16[1,16,128,130]{2,1,3,0:T(8,128)(2,1)S(1)} collective-permute-done((bf16[1,16,128,130]{2,1,3,0:T(8,128)(2,1)S(1)}, bf16[1,16,128,130]{2,1,3,0:T(8,128)(2,1)S(1)}, u32[]{:S(2)}, u32[]{:S(2)}) %collective-permute-start.11) | collective-permute-done | bytes 532512 | tf_op jit(solution)/shard_map/ppermute | solution.py:37
  84.6 3.3 %collective-permute-done.10 = bf16[1,16,128,130]{2,1,3,0:T(8,128)(2,1)} collective-permute-done((bf16[1,16,128,130]{2,1,3,0:T(8,128)(2,1)S(1)}, bf16[1,16,128,130]{2,1,3,0:T(8,128)(2,1)}, u32[]{:S(2)}, u32[]{:S(2)}) %collective-permute-start.10) | collective-permute-done | bytes 532512 | tf_op jit(solution)/shard_map/ppermute | solution.py:34
  94.2 4.4 %collective-permute-done.13 = bf16[3,1,128,130]{3,2,1,0:T(8,128)(2,1)S(1)} collective-permute-done((bf16[3,1,128,130]{3,2,1,0:T(8,128)(2,1)S(1)}, bf16[3,1,128,130]{3,2,1,0:T(8,128)(2,1)S(1)}, u32[]{:S(2)}, u32[]{:S(2)}) %collective-permute-start.13) | collective-permute-done | bytes 99872 | tf_op jit(solution)/shard_map/ppermute | solution.py:37
  98.6 2.3 %maximum_bitcast_fusion.1 = bf16[3,18,128,1,130]{4,2,1,0,3:T(8,128)(2,1)} fusion(bf16[3,1,128,130]{3,2,1,0:T(8,128)(2,1)S(1)} %collective-permute-done.13, bf16[1,16,128,130]{3,2,1,0:T(8,128)(2,1)S(1)} %copy.102, bf16[1,16,128,130]{3,2,1,0:T(8,128)(2,1)S(1)} %pad.8, bf16[1,16,128,130]{3,2,1,0:T(8,128)(2,1)S(1)} %copy.101, ...), kind=kLoop, calls=%fused_computation.6 | loop fusion | flops 3594240 | bytes 3594240 | tf_op jit(solution)/shard_map/broadcast_in_dim | solution.py:44
  100.9 4.0 %copy.111 = bf16[3,18,128,1,130]{2,4,1,0,3:T(8,128)(2,1)S(1)} copy(bf16[3,18,128,1,130]{4,2,1,0,3:T(8,128)(2,1)} %maximum_bitcast_fusion.1) | data formatting | bytes 3594240
  106.3 3.3 %reshape.116 = bf16[3,18,128,1,8,17]{2,5,4,1,0,3:T(8,128)(2,1)S(1)} reshape(bf16[3,18,128,1,136]{2,4,1,0,3:T(8,128)(2,1)} %pad.11.clone) | data formatting | bytes 3760128 | tf_op jit(solution)/shard_map/conv_general_dilated | solution.py:43
  110.6 4.2 %fusion.16 = f32[1,16,8,17,32]{4,2,3,1,0:T(8,128)S(1)} fusion(bf16[3,3,3,32,128]{4,3,2,1,0:T(8,128)(2,1)S(1)} %copy-done.3, bf16[3,18,128,1,7,2]{2,4,5,1,0,3:T(8,128)(2,1)S(1)} %slice.28, bf16[3,18,128,1,8,17]{2,4,5,1,0,3:T(8,128)(2,1)S(1)} %copy.105, pred[8,17]{0,1:T(8,128)(4,1)S(1)} %copy-done.4), kind=kOutput, calls=%fused_computation.19 | convolution fusion | flops 487669760 | bytes 2573448 | tf_op jit(solution)/shard_map/conv_general_dilated | solution.py:43
  (57 shorter events, 28.8 us)
Async XLA Ops:
  0.0 54.5 %copy-start = (bf16[3,3,3,32,128]{4,3,2,1,0:T(8,128)(2,1)S(1)}, bf16[3,3,3,32,128]{4,3,2,1,0:T(8,128)(2,1)}, u32[]{:S(2)}) copy-start(bf16[3,3,3,32,128]{4,3,2,1,0:T(8,128)(2,1)} %param.6) | copy-start | bytes 663556
  0.0 8.4 %collective-permute-start = (bf16[1,16,32,128]{3,2,1,0:T(8,128)(2,1)}, bf16[1,16,32,128]{3,2,1,0:T(8,128)(2,1)S(1)}, u32[]{:S(2)}, u32[]{:S(2)}) collective-permute-start(bf16[1,16,32,128]{3,2,1,0:T(8,128)(2,1)} %param.5), channel_id=1, source_target_pairs={{0,1},{1,2},{2,3},{3,0},{4,5},{5,6},{6,7},{7,4},{8,9},{9,10},{10,1... | collective-permute-start | bytes 393224 | tf_op jit(solution)/shard_map/ppermute | solution.py:20
  1.6 8.0 %collective-permute-start.2 = (bf16[1,16,32,128]{3,2,1,0:T(8,128)(2,1)}, bf16[1,16,32,128]{3,2,1,0:T(8,128)(2,1)S(1)}, u32[]{:S(2)}, u32[]{:S(2)}) collective-permute-start(bf16[1,16,32,128]{3,2,1,0:T(8,128)(2,1)} %param.5), channel_id=1, source_target_pairs={{1,0},{2,1},{3,2},{0,3},{5,4},{6,5},{7,6},{4,7},{9,8},{10,9},{11,1... | collective-permute-start | bytes 393224 | tf_op jit(solution)/shard_map/ppermute | solution.py:22
  8.4 6.8 %collective-permute-start.1 = (bf16[1,16,32,128]{3,2,1,0:T(8,128)(2,1)S(1)}, bf16[1,16,32,128]{3,2,1,0:T(8,128)(2,1)S(1)}, u32[]{:S(2)}, u32[]{:S(2)}) collective-permute-start(bf16[1,16,32,128]{3,2,1,0:T(8,128)(2,1)S(1)} %collective-permute-done), channel_id=1, source_target_pairs={{0,1},{1,2},{2,3},{3,0},{4,5},{5,6},{6,7},{7,4},{8,9},{9,10},{10,1... | collective-permute-start | bytes 393224 | tf_op jit(solution)/shard_map/ppermute | solution.py:20
  17.9 8.7 %collective-permute-start.4 = (bf16[1,16,128,130]{2,1,3,0:T(8,128)(2,1)S(1)}, bf16[1,16,128,130]{2,1,3,0:T(8,128)(2,1)S(1)}, u32[]{:S(2)}, u32[]{:S(2)}) collective-permute-start(bf16[1,16,128,130]{2,1,3,0:T(8,128)(2,1)S(1)} %copy.87), channel_id=1, source_target_pairs={{8,0},{16,8},{24,16},{9,1},{17,9},{25,17},{10,2},{18,10},{26,18},{... | collective-permute-start | bytes 1597448 | tf_op jit(solution)/shard_map/ppermute | solution.py:37
  19.8 10.7 %collective-permute-start.3 = (bf16[1,16,128,130]{2,1,3,0:T(8,128)(2,1)S(1)}, bf16[1,16,128,130]{2,1,3,0:T(8,128)(2,1)}, u32[]{:S(2)}, u32[]{:S(2)}) collective-permute-start(bf16[1,16,128,130]{2,1,3,0:T(8,128)(2,1)S(1)} %copy.87), channel_id=1, source_target_pairs={{0,8},{8,16},{16,24},{1,9},{9,17},{17,25},{2,10},{10,18},{18,26},{... | collective-permute-start | bytes 1597448 | tf_op jit(solution)/shard_map/ppermute | solution.py:34
  32.1 6.6 %collective-permute-start.5 = (bf16[3,1,128,130]{3,2,1,0:T(8,128)(2,1)S(1)}, bf16[3,1,128,130]{3,2,1,0:T(8,128)(2,1)S(1)}, u32[]{:S(2)}, u32[]{:S(2)}) collective-permute-start(bf16[3,1,128,130]{3,2,1,0:T(8,128)(2,1)S(1)} %get-tuple-element.7), channel_id=1, source_target_pairs={{0,4},{1,5},{2,6},{3,7},{8,12},{9,13},{10,14},{11,15},{16,20},{17,... | collective-permute-start | bytes 299528 | tf_op jit(solution)/shard_map/ppermute | solution.py:34
  35.5 7.6 %collective-permute-start.6 = (bf16[3,1,128,130]{3,2,1,0:T(8,128)(2,1)S(1)}, bf16[3,1,128,130]{3,2,1,0:T(8,128)(2,1)S(1)}, u32[]{:S(2)}, u32[]{:S(2)}) collective-permute-start(bf16[3,1,128,130]{3,2,1,0:T(8,128)(2,1)S(1)} %get-tuple-element.8), channel_id=1, source_target_pairs={{4,0},{5,1},{6,2},{7,3},{12,8},{13,9},{14,10},{15,11},{20,16},{21,... | collective-permute-start | bytes 299528 | tf_op jit(solution)/shard_map/ppermute | solution.py:37
  54.1 0.7 copy-start.1
  54.1 0.7 copy-start.4
  59.9 6.8 %collective-permute-start.7 = (bf16[1,16,32,128]{3,2,1,0:T(8,128)(2,1)S(1)}, bf16[1,16,32,128]{3,2,1,0:T(8,128)(2,1)S(1)}, u32[]{:S(2)}, u32[]{:S(2)}) collective-permute-start(bf16[1,16,32,128]{3,2,1,0:T(8,128)(2,1)S(1)} %fusion.27), channel_id=1, source_target_pairs={{0,1},{1,2},{2,3},{3,0},{4,5},{5,6},{6,7},{7,4},{8,9},{9,10},{10,1... | collective-permute-start | bytes 393224 | tf_op jit(solution)/shard_map/ppermute | solution.py:20
  59.9 7.2 %collective-permute-start.9 = (bf16[1,16,32,128]{3,2,1,0:T(8,128)(2,1)S(1)}, bf16[1,16,32,128]{3,2,1,0:T(8,128)(2,1)S(1)}, u32[]{:S(2)}, u32[]{:S(2)}) collective-permute-start(bf16[1,16,32,128]{3,2,1,0:T(8,128)(2,1)S(1)} %fusion.27), channel_id=1, source_target_pairs={{1,0},{2,1},{3,2},{0,3},{5,4},{6,5},{7,6},{4,7},{9,8},{10,9},{11,1... | collective-permute-start | bytes 393224 | tf_op jit(solution)/shard_map/ppermute | solution.py:22
  66.7 6.8 %collective-permute-start.8 = (bf16[1,16,32,128]{3,2,1,0:T(8,128)(2,1)S(1)}, bf16[1,16,32,128]{3,2,1,0:T(8,128)(2,1)S(1)}, u32[]{:S(2)}, u32[]{:S(2)}) collective-permute-start(bf16[1,16,32,128]{3,2,1,0:T(8,128)(2,1)S(1)} %collective-permute-done.7), channel_id=1, source_target_pairs={{0,1},{1,2},{2,3},{3,0},{4,5},{5,6},{6,7},{7,4},{8,9},{9,10},{10,1... | collective-permute-start | bytes 393224 | tf_op jit(solution)/shard_map/ppermute | solution.py:20
  75.3 8.7 %collective-permute-start.11 = (bf16[1,16,128,130]{2,1,3,0:T(8,128)(2,1)S(1)}, bf16[1,16,128,130]{2,1,3,0:T(8,128)(2,1)S(1)}, u32[]{:S(2)}, u32[]{:S(2)}) collective-permute-start(bf16[1,16,128,130]{2,1,3,0:T(8,128)(2,1)S(1)} %copy.99), channel_id=1, source_target_pairs={{8,0},{16,8},{24,16},{9,1},{17,9},{25,17},{10,2},{18,10},{26,18},{... | collective-permute-start | bytes 1597448 | tf_op jit(solution)/shard_map/ppermute | solution.py:37
  77.2 10.7 %collective-permute-start.10 = (bf16[1,16,128,130]{2,1,3,0:T(8,128)(2,1)S(1)}, bf16[1,16,128,130]{2,1,3,0:T(8,128)(2,1)}, u32[]{:S(2)}, u32[]{:S(2)}) collective-permute-start(bf16[1,16,128,130]{2,1,3,0:T(8,128)(2,1)S(1)} %copy.99), channel_id=1, source_target_pairs={{0,8},{8,16},{16,24},{1,9},{9,17},{17,25},{2,10},{10,18},{18,26},{... | collective-permute-start | bytes 1597448 | tf_op jit(solution)/shard_map/ppermute | solution.py:34
  89.5 4.7 %collective-permute-start.12 = (bf16[3,1,128,130]{3,2,1,0:T(8,128)(2,1)S(1)}, bf16[3,1,128,130]{3,2,1,0:T(8,128)(2,1)S(1)}, u32[]{:S(2)}, u32[]{:S(2)}) collective-permute-start(bf16[3,1,128,130]{3,2,1,0:T(8,128)(2,1)S(1)} %get-tuple-element.5), channel_id=1, source_target_pairs={{0,4},{1,5},{2,6},{3,7},{8,12},{9,13},{10,14},{11,15},{16,20},{17,... | collective-permute-start | bytes 299528 | tf_op jit(solution)/shard_map/ppermute | solution.py:34
  91.1 7.6 %collective-permute-start.13 = (bf16[3,1,128,130]{3,2,1,0:T(8,128)(2,1)S(1)}, bf16[3,1,128,130]{3,2,1,0:T(8,128)(2,1)S(1)}, u32[]{:S(2)}, u32[]{:S(2)}) collective-permute-start(bf16[3,1,128,130]{3,2,1,0:T(8,128)(2,1)S(1)} %get-tuple-element.6), channel_id=1, source_target_pairs={{4,0},{5,1},{6,2},{7,3},{12,8},{13,9},{14,10},{15,11},{20,16},{21,... | collective-permute-start | bytes 299528 | tf_op jit(solution)/shard_map/ppermute | solution.py:37
  109.7 0.9 copy-start.3
  115.1 0.7 copy-start.2
